TPU v7x, 32 devices: a whole 2x2x4 slice. The times are simulated.
32 devices in a mesh: scene: 4 (over x, core), seq: 8 (over z, y).
Axes of the slice: x: 2, y: 2, z: 4, core: 2. Of those that a mesh axis runs over, the one named last changes fastest.
Arguments:
- tokens: bfloat16 [10240, 768], P(('scene', 'seq')), may hold values from -6 to 6
- scene_tokens: int32 [4], P('scene'), may hold values from 128 to 320, as said below
- cotangent: bfloat16 [10240, 768], P(('scene', 'seq')), may hold values from -6 to 6
- qkv_master: float32 [768, 2304], P(('scene', 'seq')), may hold values from -0.21875 to 0.21875
- out_master: float32 [768, 768], P(('scene', 'seq')), may hold values from -6 to 6
- up_master: float32 [768, 3072], P(('scene', 'seq')), may hold values from -0.21875 to 0.21875
- down_master: float32 [3072, 768], P(('scene', 'seq')), may hold values from -0.109375 to 0.109375
- gain_one: float32 [768], replicated, may hold values from 0.5 to 1.5
- gain_two: float32 [768], replicated, may hold values from 0.5 to 1.5
Outputs:
- mixed: bfloat16 [10240, 768], P(('scene', 'seq'))
- input_grad: float32 [10240, 768], P(('scene', 'seq'))
- qkv_grad: float32 [768, 2304], P(('scene', 'seq'))
- out_grad: float32 [768, 768], P(('scene', 'seq'))
- up_grad: float32 [768, 3072], P(('scene', 'seq'))
- down_grad: float32 [3072, 768], P(('scene', 'seq'))
- gain_one_grad: float32 [768], P(('scene', 'seq'))
- gain_two_grad: float32 [768], P(('scene', 'seq'))
Inputs may be any that keep to these rules, and one draw needn't show every extreme that they name: Slots 0 to scene_tokens[s] - 1 of every device of scene s's group hold that scene's tokens, the others are padding; one scene, drawn from the seed, has all 320 slots of every device live.
All inputs are finite; a program needn't handle non-finite values.
Results may differ from a plain program's by a relative error of at most 0.02.
Values may be sent and summed in bfloat16 or wider, within the bound.
No kernel may reach another device: no remote copies, remote signals or barrier semaphores. Data moves between devices by JAX's collectives and lax.ppermute only.
A program may use at most 512 MiB of HBM per device.

v0:
```python
import jax
import jax.numpy as jnp
from jax import lax
from jax.sharding import PartitionSpec as P

HEADS = 12
HEAD = 64
NEG_BIG = -1e30


def norm_rows(values, gain_vector):
    mean_value = jnp.mean(values, axis=-1, keepdims=True)
    centered = values - mean_value
    variance = jnp.mean(centered * centered, axis=-1, keepdims=True)
    inverse = lax.rsqrt(variance + 1e-05)
    scaled = centered * inverse
    return (scaled * gain_vector, scaled, inverse)


def norm_back(grad_result, scaled, inverse, gain_vector):
    grad_scaled = grad_result * gain_vector
    first_mean = jnp.mean(grad_scaled, axis=-1, keepdims=True)
    second_mean = jnp.mean(grad_scaled * scaled, axis=-1, keepdims=True)
    grad_input = inverse * (grad_scaled - first_mean - scaled * second_mean)
    return (grad_input, jnp.sum(grad_result * scaled, axis=0))


def split_heads(values):
    return values.reshape(values.shape[0], HEADS, HEAD)


def score_grads(query_part, grad_part, key_part, value_part, lse_part, delta_part, live_keys):
    scores = (
        jnp.einsum("qhd,khd->hqk", query_part, key_part, preferred_element_type=jnp.float32) * 0.125
    )
    weights_now = jnp.where(live_keys[None, None, :], jnp.exp(scores - lse_part[:, :, None]), 0.0)
    grad_weights = jnp.einsum(
        "qhd,khd->hqk", grad_part, value_part, preferred_element_type=jnp.float32
    )
    dscore = (weights_now * (grad_weights - delta_part[:, :, None])).astype(jnp.bfloat16)
    return (weights_now.astype(jnp.bfloat16), dscore)


def on_device(
    tokens,
    scene_tokens,
    cotangent,
    qkv_master,
    out_master,
    up_master,
    down_master,
    gain_one,
    gain_two,
):
    local_rows = tokens.shape[0]
    model_width = tokens.shape[1]
    live_count = scene_tokens[0]
    local_live = jnp.arange(local_rows, dtype=jnp.int32) < live_count
    qkv_part = qkv_master.astype(jnp.bfloat16)
    out_part = out_master.astype(jnp.bfloat16)
    up_part = up_master.astype(jnp.bfloat16)
    down_part = down_master.astype(jnp.bfloat16)
    qkv_weight, out_weight, up_weight, down_weight = (
        lax.all_gather(qkv_part, ("scene", "seq"), axis=0, tiled=True),
        lax.all_gather(out_part, ("scene", "seq"), axis=0, tiled=True),
        lax.all_gather(up_part, ("scene", "seq"), axis=0, tiled=True),
        lax.all_gather(down_part, ("scene", "seq"), axis=0, tiled=True),
    )
    inputs = tokens.astype(jnp.float32)
    normed_one, scaled_one, inverse_one = norm_rows(inputs, gain_one)
    normed_low = normed_one.astype(jnp.bfloat16)
    qkv_rows = jnp.dot(normed_low, qkv_weight, preferred_element_type=jnp.float32).astype(
        jnp.bfloat16
    )
    queries = qkv_rows[:, :model_width]
    key_rows = qkv_rows[:, model_width : 2 * model_width]
    value_rows = qkv_rows[:, 2 * model_width :]
    query_heads = split_heads(queries)

    def piece_live(piece_rows):
        places = jnp.arange(piece_rows, dtype=jnp.int32)
        return places % local_rows < live_count

    row_max = jnp.full((HEADS, local_rows), NEG_BIG, jnp.float32)
    key_piece = lax.all_gather(key_rows, "seq", axis=0, tiled=True)
    value_piece = lax.all_gather(value_rows, "seq", axis=0, tiled=True)
    piece_rows = key_piece.shape[0]
    scores = (
        jnp.einsum(
            "qhd,khd->hqk", query_heads, split_heads(key_piece), preferred_element_type=jnp.float32
        )
        * 0.125
    )
    scores = jnp.where(piece_live(piece_rows)[None, None, :], scores, NEG_BIG)
    new_max = jnp.maximum(row_max, jnp.max(scores, axis=-1))
    exponent = jnp.exp(scores - new_max[:, :, None])
    new_sum = jnp.sum(exponent, axis=-1)
    update = jnp.einsum(
        "hqk,khd->hqd",
        exponent.astype(jnp.bfloat16),
        split_heads(value_piece),
        preferred_element_type=jnp.float32,
    )
    row_lse = new_max + jnp.log(new_sum)
    attended = (
        (update / new_sum[:, :, None])
        .transpose(1, 0, 2)
        .reshape(local_rows, model_width)
        .astype(jnp.bfloat16)
    )
    resid = inputs + jnp.dot(attended, out_weight, preferred_element_type=jnp.float32)
    normed_two, scaled_two, inverse_two = norm_rows(resid, gain_two)
    normed_two_low = normed_two.astype(jnp.bfloat16)
    upper = jnp.dot(normed_two_low, up_weight, preferred_element_type=jnp.float32)
    activated, gelu_back = jax.vjp(jax.nn.gelu, upper)
    activated_low = activated.astype(jnp.bfloat16)
    mixed = (
        resid + jnp.dot(activated_low, down_weight, preferred_element_type=jnp.float32)
    ).astype(jnp.bfloat16)
    grad_result = cotangent.astype(jnp.float32) * local_live[:, None].astype(jnp.float32)
    grad_low = grad_result.astype(jnp.bfloat16)
    down_grad = jnp.einsum("tf,td->fd", activated_low, grad_low, preferred_element_type=jnp.float32)
    grad_active = jnp.einsum("td,fd->tf", grad_low, down_weight, preferred_element_type=jnp.float32)
    grad_upper = gelu_back(grad_active)[0].astype(jnp.bfloat16)
    up_grad = jnp.einsum(
        "td,tf->df", normed_two_low, grad_upper, preferred_element_type=jnp.float32
    )
    grad_normed_two = jnp.einsum(
        "tf,df->td", grad_upper, up_weight, preferred_element_type=jnp.float32
    )
    grad_norm_second, gain_two_grad = norm_back(grad_normed_two, scaled_two, inverse_two, gain_two)
    grad_resid = grad_result + grad_norm_second
    grad_branch = grad_resid.astype(jnp.bfloat16)
    out_grad = jnp.einsum("te,td->ed", attended, grad_branch, preferred_element_type=jnp.float32)
    grad_attended = jnp.einsum(
        "td,ed->te", grad_branch, out_weight, preferred_element_type=jnp.float32
    ).astype(jnp.bfloat16)
    grad_heads = split_heads(grad_attended)
    delta = jnp.sum(
        grad_heads.astype(jnp.float32) * split_heads(attended).astype(jnp.float32), axis=-1
    ).T
    total_rows = local_rows * lax.axis_size("seq")
    key_piece = lax.all_gather(key_rows, "seq", axis=0, tiled=True)
    value_piece = lax.all_gather(value_rows, "seq", axis=0, tiled=True)
    piece_rows = key_piece.shape[0]
    key_heads = split_heads(key_piece)
    weights_low, dscore = score_grads(
        query_heads,
        grad_heads,
        key_heads,
        split_heads(value_piece),
        row_lse,
        delta,
        piece_live(piece_rows),
    )
    grad_query = (
        jnp.einsum("hqk,khd->qhd", dscore, key_heads, preferred_element_type=jnp.float32) * 0.125
    )
    key_terms = (
        jnp.einsum("hqk,qhd->khd", dscore, query_heads, preferred_element_type=jnp.float32) * 0.125
    )
    value_terms = jnp.einsum(
        "hqk,qhd->khd", weights_low, grad_heads, preferred_element_type=jnp.float32
    )
    key_buffer = key_terms
    value_buffer = value_terms
    grad_query, key_buffer, value_buffer = (grad_query, key_buffer, value_buffer)
    grad_keys, grad_values = (
        lax.psum_scatter(
            key_buffer.reshape(total_rows, model_width).astype(jnp.bfloat16),
            "seq",
            scatter_dimension=0,
            tiled=True,
        ).astype(jnp.float32),
        lax.psum_scatter(
            value_buffer.reshape(total_rows, model_width).astype(jnp.bfloat16),
            "seq",
            scatter_dimension=0,
            tiled=True,
        ).astype(jnp.float32),
    )
    grad_qkv = jnp.concatenate(
        [grad_query.reshape(local_rows, model_width), grad_keys, grad_values], axis=1
    ).astype(jnp.bfloat16)
    qkv_grad = jnp.einsum("td,te->de", normed_low, grad_qkv, preferred_element_type=jnp.float32)
    grad_normed_one = jnp.einsum(
        "te,de->td", grad_qkv, qkv_weight, preferred_element_type=jnp.float32
    )
    grad_norm_first, gain_one_grad = norm_back(grad_normed_one, scaled_one, inverse_one, gain_one)
    input_grad = grad_resid + grad_norm_first
    qkv_share, out_share, up_share, down_share, first_share, second_share = (
        lax.psum_scatter(qkv_grad, ("scene", "seq"), scatter_dimension=0, tiled=True),
        lax.psum_scatter(out_grad, ("scene", "seq"), scatter_dimension=0, tiled=True),
        lax.psum_scatter(up_grad, ("scene", "seq"), scatter_dimension=0, tiled=True),
        lax.psum_scatter(down_grad, ("scene", "seq"), scatter_dimension=0, tiled=True),
        lax.psum_scatter(gain_one_grad, ("scene", "seq"), scatter_dimension=0, tiled=True),
        lax.psum_scatter(gain_two_grad, ("scene", "seq"), scatter_dimension=0, tiled=True),
    )
    return (
        mixed,
        input_grad,
        qkv_share,
        out_share,
        up_share,
        down_share,
        first_share,
        second_share,
    )


def solution(mesh):
    in_specs = (
        P(("scene", "seq"), None),
        P("scene"),
        P(("scene", "seq"), None),
        P(("scene", "seq"), None),
        P(("scene", "seq"), None),
        P(("scene", "seq"), None),
        P(("scene", "seq"), None),
        P(),
        P(),
    )
    out_specs = (
        P(("scene", "seq"), None),
        P(("scene", "seq"), None),
        P(("scene", "seq"), None),
        P(("scene", "seq"), None),
        P(("scene", "seq"), None),
        P(("scene", "seq"), None),
        P(("scene", "seq")),
        P(("scene", "seq")),
    )
    return jax.shard_map(
        on_device, mesh=mesh, in_specs=in_specs, out_specs=out_specs, check_vma=False
    )
```

profile of v0, /device:TPU:0, one launch (start us, length us, event | category | flops | bytes accessed | tf_op | source)
XLA Modules:
  0.0 1135.8 jit_solution(7848209360860348284)
XLA Ops:
  7.2 1.6 convert_element_type.98
  8.9 1.2 convert_reduce_fusion
  10.1 1.3 fusion.36
  11.4 63.0 %all-gather.7.cloned.1.call-done = bf16[768,2304]{1,0:T(8,128)(2,1)} async-done(((bf16[24,2304]{1,0:T(8,128)(2,1)}), bf16[768,2304]{1,0:T(8,128)(2,1)}) %all-gather.7.cloned.1.call-update) | async-done | bytes 3538960 | tf_op jit(solution)/shard_map/all_gather | solution.py:64
  74.4 3.6 convolution_convert_fusion
  78.0 1.0 fusion.66
  79.1 0.7 all-gather.11.cloned.1.call-update
  81.3 0.7 convert_element_type.107
  83.1 65.0 %all-gather.9.cloned.1.call-done = bf16[2560,768]{1,0:T(8,128)(2,1)} async-done(((bf16[320,768]{1,0:T(8,128)(2,1)}), bf16[2560,768]{1,0:T(8,128)(2,1)}) %all-gather.9.cloned.1.call-update) | async-done | bytes 3932176 | tf_op jit(solution)/shard_map/all_gather | solution.py:85
  148.1 6.3 copy.29
  154.4 17.1 %select_reduce_fusion = (f32[12,320]{1,0:T(8,128)S(1)}, f32[12,320,2560]{2,1,0:T(8,128)}) fusion(pred[2560]{0:T(1024)(128)(4,1)S(1)} %fusion.51, bf16[320,12,64]{0,2,1:T(8,128)(2,1)S(1)} %bitcast.50, bf16[2560,12,64]{0,2,1:T(8,128)(2,1)} %bitcast.47), kind=kOutput, calls=%fused_computation.3 | convolution fusion | flops 1287778560 | bytes 43763200 | tf_op jit(solution)/shard_map/qhd,khd->hqk/dot_general | solution.py:89
  171.5 47.9 %all-gather.11.cloned.1.call-done = bf16[2560,768]{1,0:T(8,128)(2,1)} async-done(((bf16[320,768]{1,0:T(8,128)(2,1)}), bf16[2560,768]{1,0:T(8,128)(2,1)}) %all-gather.11.cloned.1.call-update) | async-done | bytes 3932176 | tf_op jit(solution)/shard_map/all_gather | solution.py:86
  219.4 6.2 copy.30
  225.6 18.1 %fusion = f32[12,320]{1,0:T(8,128)S(1)} fusion(f32[12,320,2560]{2,1,0:T(8,128)} %get-tuple-element.20, f32[12,320]{1,0:T(8,128)S(1)} %broadcast_maximum_fusion, pred[2560]{0:T(1024)(128)(4,1)S(1)} %fusion.51), kind=kLoop, calls=%fused_computation.4 | loop fusion | flops 39317760 | bytes 39354880 | tf_op jit(solution)/shard_map/reduce_sum | solution.py:97
  243.8 15.2 %divide_convert_fusion = bf16[320,12,64]{0,2,1:T(8,128)(2,1)S(1)} fusion(bf16[2560,12,64]{0,2,1:T(8,128)(2,1)S(1)} %bitcast.55, f32[12,320,2560]{2,1,0:T(8,128)} %get-tuple-element.20, f32[12,320]{1,0:T(8,128)S(1)} %broadcast_maximum_fusion, pred[2560]{0:T(1024)(128)(4,1)S(1)} %fusion.51, f32[320,12]{0,1:T(8,128)S(1)} %bitcast.62), kind=kOutput, calls=%fused_computation.35 | convolution fusion | flops 1298104320 | bytes 43778560 | tf_op jit(solution)/shard_map/hqk,khd->hqd/dot_general | solution.py:98
  259.0 16.4 %all-gather.13.cloned.1.call-done = bf16[768,768]{1,0:T(8,128)(2,1)} async-done(((bf16[24,768]{1,0:T(8,128)(2,1)}), bf16[768,768]{1,0:T(8,128)(2,1)}) %all-gather.13.cloned.1.call-update) | async-done | bytes 1179664 | tf_op jit(solution)/shard_map/all_gather | solution.py:65
  275.4 1.9 fusion.67
  278.2 63.0 %all-gather.15.cloned.1.call-done = bf16[768,3072]{1,0:T(8,128)(2,1)} async-done(((bf16[24,3072]{1,0:T(8,128)(2,1)}), bf16[768,3072]{1,0:T(8,128)(2,1)}) %all-gather.15.cloned.1.call-update) | async-done | bytes 4718608 | tf_op jit(solution)/shard_map/all_gather | solution.py:66
  341.3 6.0 fusion.65
  347.3 59.8 %all-gather.17.cloned.1.call-done = bf16[3072,768]{1,0:T(8,128)(2,1)} async-done(((bf16[96,768]{1,0:T(8,128)(2,1)}), bf16[3072,768]{1,0:T(8,128)(2,1)}) %all-gather.17.cloned.1.call-update) | async-done | bytes 4718608 | tf_op jit(solution)/shard_map/all_gather | solution.py:67
  407.1 7.8 fusion.18
  415.0 2.5 multiply_reduce_fusion.1
  418.5 1.1 copy.31
  419.5 18.2 %fusion.9 = bf16[12,64,2560]{2,1,0:T(8,128)(2,1)} fusion(bf16[320,12,64]{0,2,1:T(8,128)(2,1)} %bitcast.59, f32[12,320,2560]{2,1,0:T(8,128)} %get-tuple-element.20, f32[12,320]{1,0:T(8,128)} %log_add_fusion, pred[2560]{0:T(1024)(128)(4,1)S(1)} %fusion.51), kind=kOutput, calls=%fused_computation.14 | convolution fusion | flops 1299578880 | bytes 43763200 | tf_op jit(solution)/shard_map/hqk,qhd->khd/dot_general | solution.py:162
  437.7 6.3 copy.34
  444.1 1.4 multiply_reduce_fusion
  445.6 26.5 %multiply_convert_fusion = bf16[12,320,2560]{2,1,0:T(8,128)(2,1)} fusion(f32[12,320,2560]{2,1,0:T(8,128)} %get-tuple-element.20, bf16[320,12,64]{0,2,1:T(8,128)(2,1)} %bitcast.61, bf16[2560,12,64]{0,2,1:T(8,128)(2,1)} %bitcast.54, f32[12,320]{1,0:T(8,128)S(1)} %bitcast.63, f32[12,320]{1,0:T(8,128)S(1)} %copy-done.19, pred[2560]{0:T(1024)(128)(4,1)S(1)} %fusion.51), kind=kOutput, calls=%fused_computation | convolution fusion | flops 1317273600 | bytes 63439360 | tf_op jit(solution)/shard_map/qhd,khd->hqk/dot_general | solution.py:37
  472.1 12.6 %multiply_convert_fusion.1 = bf16[12,64,2560]{2,1,0:T(8,128)(2,1)} fusion(bf16[320,12,64]{0,2,1:T(8,128)(2,1)S(1)} %bitcast.51, bf16[12,320,2560]{2,1,0:T(8,128)(2,1)} %multiply_convert_fusion), kind=kOutput, calls=%fused_computation.11 | convolution fusion | flops 1262223360 | bytes 24084480 | tf_op jit(solution)/shard_map/hqk,qhd->khd/dot_general | solution.py:160
  484.7 6.3 copy.32
  491.1 1.0 copy-done.2
  492.1 2.2 fusion.42
  494.3 6.8 fusion.64
  501.2 1.0 copy-done.9
  502.2 8.7 fusion.45
  511.0 10.9 fusion.23
  522.0 5.4 reduce-scatter.21.cloned.1.call-done
  527.4 2.1 copy.35
  529.5 86.1 %reduce-scatter.19.cloned.1.call-done = bf16[320,768]{1,0:T(8,128)(2,1)} async-done(((bf16[2560,768]{1,0:T(8,128)(2,1)}), bf16[320,768]{1,0:T(8,128)(2,1)}) %reduce-scatter.19.cloned.1.call-update) | async-done | bytes 491536
  615.6 2.1 copy.33
  617.7 6.4 fusion.38
  624.1 6.9 fusion.22
  631.0 1.9 fusion.35
  632.9 40.4 %all-reduce.2 = (f32[768]{0:T(1024)S(1)}, f32[768]{0:T(1024)S(1)}) all-reduce(f32[768]{0:T(1024)S(1)} %get-tuple-element.10, f32[768]{0:T(1024)S(1)} %copy-done.23), channel_id=8, replica_groups=mesh['scene'=4,'seq'=8] {'scene','seq'}, use_global_device_ids=true, to_apply=%region_18.19.clone | all-reduce | flops 1536 | bytes 12288
  674.5 1.3 fusion.34
  675.8 44.5 %reduce-scatter.13.cloned.1.call-done = f32[24,768]{1,0:T(8,128)} async-done(((f32[768,768]{1,0:T(8,128)}), f32[24,768]{1,0:T(8,128)}) %reduce-scatter.13.cloned.1.call-update) | async-done | bytes 73744 | tf_op jit(solution)/shard_map/reduce_scatter | solution.py:193
  720.3 142.0 %reduce-scatter.15.cloned.1.call-done = f32[24,3072]{1,0:T(8,128)} async-done(((f32[768,3072]{1,0:T(8,128)}), f32[24,3072]{1,0:T(8,128)}) %reduce-scatter.15.cloned.1.call-update) | async-done | bytes 294928 | tf_op jit(solution)/shard_map/reduce_scatter | solution.py:194
  862.3 141.0 %reduce-scatter.17.cloned.1.call-done = f32[96,768]{1,0:T(8,128)} async-done(((f32[3072,768]{1,0:T(8,128)}), f32[96,768]{1,0:T(8,128)}) %reduce-scatter.17.cloned.1.call-update) | async-done | bytes 294928 | tf_op jit(solution)/shard_map/reduce_scatter | solution.py:195
  1003.3 125.4 %reduce-scatter.11.cloned.1.call-done = f32[24,2304]{1,0:T(8,128)} async-done(((f32[768,2304]{1,0:T(8,128)}), f32[24,2304]{1,0:T(8,128)}) %reduce-scatter.11.cloned.1.call-update) | async-done | bytes 221200 | tf_op jit(solution)/shard_map/reduce_scatter | solution.py:192
  (92 shorter events, 5.5 us)
Async XLA Ops:
  7.2 67.2 %all-gather.7.cloned.1.call-start = ((), (), s32[]{:S(2)}) async-start(), calls=%async_computation.6 | async-start | bytes 3649536 | tf_op jit(solution)/shard_map/all_gather | solution.py:64
  8.8 139.3 %all-gather.9.cloned.1.call-start = ((), (), s32[]{:S(2)}) async-start(), calls=%async_computation.7 | async-start | bytes 4423680 | tf_op jit(solution)/shard_map/all_gather | solution.py:85
  10.1 64.3 %copy-start.15 = (f32[320]{0:T(512)}, f32[320]{0:T(512)S(1)}, u32[]{:S(2)}) copy-start(f32[320]{0:T(512)S(1)} %broadcast_multiply_fusion.5) | copy-start | bytes 3844
  11.4 63.0 %copy-start.17 = (f32[320]{0:T(512)}, f32[320]{0:T(512)S(1)}, u32[]{:S(2)}) copy-start(f32[320]{0:T(512)S(1)} %add_rsqrt_fusion.1) | copy-start | bytes 3844
  78.0 1.9 copy-start.14
  78.0 2.6 copy-start.10
  78.0 3.3 copy-start.11
  79.1 140.3 %all-gather.11.cloned.1.call-start = ((), (), s32[]{:S(2)}) async-start(), calls=%async_computation.8 | async-start | bytes 4423680 | tf_op jit(solution)/shard_map/all_gather | solution.py:86
  79.8 195.6 %all-gather.13.cloned.1.call-start = ((), (), s32[]{:S(2)}) async-start(), calls=%async_computation.9 | async-start | bytes 1216512 | tf_op jit(solution)/shard_map/all_gather | solution.py:65
  80.5 260.8 %all-gather.15.cloned.1.call-start = ((), (), s32[]{:S(2)}) async-start(), calls=%async_computation.10 | async-start | bytes 4866048 | tf_op jit(solution)/shard_map/all_gather | solution.py:66
  81.3 325.8 %all-gather.17.cloned.1.call-start = ((), (), s32[]{:S(2)}) async-start(), calls=%async_computation.11 | async-start | bytes 4866048 | tf_op jit(solution)/shard_map/all_gather | solution.py:67
  82.0 445.4 %reduce-scatter.21.cloned.1.call-start = ((), (), s32[]{:S(2)}) async-start(), calls=%async_computation.17 | async-start | bytes 4423680
  82.8 324.4 %copy-start.20 = (f32[320]{0:T(512)}, f32[320]{0:T(512)S(1)}, u32[]{:S(2)}) copy-start(f32[320]{0:T(512)S(1)} %fusion.55) | copy-start | bytes 3844
  225.6 18.1 %copy-start.4 = (bf16[2560,768]{0,1:T(8,128)(2,1)S(1)}, bf16[2560,768]{0,1:T(8,128)(2,1)}, u32[]{:S(2)}) copy-start(bf16[2560,768]{0,1:T(8,128)(2,1)} %copy.30) | copy-start | bytes 11796484
  243.7 31.6 %copy-start = (bf16[320,768]{1,0:T(8,128)(2,1)S(1)}, bf16[320,768]{1,0:T(8,128)(2,1)}, u32[]{:S(2)}) copy-start(bf16[320,768]{1,0:T(8,128)(2,1)} %param.9) | copy-start | bytes 1474564
  259.0 88.3 %copy-start.1 = (bf16[320,12,64]{0,2,1:T(8,128)(2,1)}, bf16[320,12,64]{0,2,1:T(8,128)(2,1)S(1)}, u32[]{:S(2)}) copy-start(bf16[320,12,64]{0,2,1:T(8,128)(2,1)S(1)} %divide_convert_fusion) | copy-start | bytes 1474564
  259.0 82.3 %copy-start.12 = (f32[768]{0:T(1024)S(1)}, f32[768]{0:T(1024)}, u32[]{:S(2)}) copy-start(f32[768]{0:T(1024)} %param.17) | copy-start | bytes 9220
  278.2 128.9 %copy-start.8 = (bf16[320,768]{1,0:T(8,128)(2,1)S(1)}, bf16[320,768]{1,0:T(8,128)(2,1)}, u32[]{:S(2)}) copy-start(bf16[320,768]{1,0:T(8,128)(2,1)} %param.11) | copy-start | bytes 1474564
  407.1 7.8 copy-start.24
  415.0 2.5 copy-start.7
  415.0 2.5 copy-start.21
  415.0 2.9 copy-start.3
  444.1 1.5 copy-start.19
  444.1 171.5 %reduce-scatter.19.cloned.1.call-start = ((), (), s32[]{:S(2)}) async-start(), calls=%async_computation.16 | async-start | bytes 4423680
  491.0 1.1 copy-start.2
  491.0 229.3 %reduce-scatter.13.cloned.1.call-start = ((), (), s32[]{:S(2)}) async-start(), calls=%async_computation.13 | async-start | bytes 2433024 | tf_op jit(solution)/shard_map/reduce_scatter | solution.py:193
  494.3 368.1 %reduce-scatter.15.cloned.1.call-start = ((), (), s32[]{:S(2)}) async-start(), calls=%async_computation.14 | async-start | bytes 9732096 | tf_op jit(solution)/shard_map/reduce_scatter | solution.py:194
  501.2 1.0 copy-start.9
  501.2 1.0 copy-start.22
  501.2 502.1 %reduce-scatter.17.cloned.1.call-start = ((), (), s32[]{:S(2)}) async-start(), calls=%async_computation.15 | async-start | bytes 9732096 | tf_op jit(solution)/shard_map/reduce_scatter | solution.py:195
  511.0 106.7 %copy-start.13 = (f32[768]{0:T(1024)S(1)}, f32[768]{0:T(1024)}, u32[]{:S(2)}) copy-start(f32[768]{0:T(1024)} %param.16) | copy-start | bytes 9220
  511.0 106.7 %copy-start.16 = (f32[320]{0:T(512)S(1)}, f32[320]{0:T(512)}, u32[]{:S(2)}) copy-start(f32[320]{0:T(512)} %copy-done.15) | copy-start | bytes 3844
  511.0 106.7 %copy-start.18 = (f32[320]{0:T(512)S(1)}, f32[320]{0:T(512)}, u32[]{:S(2)}) copy-start(f32[320]{0:T(512)} %copy-done.17) | copy-start | bytes 3844
  511.0 617.7 %reduce-scatter.11.cloned.1.call-start = ((), (), s32[]{:S(2)}) async-start(), calls=%async_computation.12 | async-start | bytes 7299072 | tf_op jit(solution)/shard_map/reduce_scatter | solution.py:192
  624.1 6.9 copy-start.5
  624.1 6.9 copy-start.6
  624.1 6.9 copy-start.25
  631.0 1.9 copy-start.23
Sparse Core Ops, SparseCore 0:
  11.5 62.8 all-gather.6
  79.2 68.8 all-gather.8
  150.9 68.4 all-gather.10
  222.7 52.6 all-gather.12
  278.7 62.5 all-gather.14
  344.6 62.4 all-gather.16
  444.2 83.1 reduce-scatter.20
  531.5 83.9 reduce-scatter.18
  621.4 98.8 reduce-scatter.12
  727.6 134.6 reduce-scatter.14
  868.8 134.4 reduce-scatter.16
  1010.4 118.2 reduce-scatter.10
where the time goes:
time: 1150 us; the launch traced here: 1140 us
  waiting for transfers between devices  860 us (75%)
  matrix products  156 us (14%)
  blocking collectives  40.4 us (4%)
  local copies, waits for them, and re-layouts  35 us (3%)
  other arithmetic  28.3 us (2%)
  between operations  15.4 us (1%)
    reduce_scatter x1, waiting for transfers between devices, on_device(): lax.psum_scatter(up_grad, ('scene', 'seq'), scatter_dimension=0, tiled=True)  142 us
    reduce_scatter x1, waiting for transfers between devices, on_device(): lax.psum_scatter(down_grad, ('scene', 'seq'), scatter_dimension=0, tiled=...  141 us
    reduce_scatter x1, waiting for transfers between devices, on_device(): lax.psum_scatter(qkv_grad, ('scene', 'seq'), scatter_dimension=0, tiled=T...  125 us
    unnamed x14, waiting for transfers between devices  92.4 us
    all_gather x1, waiting for transfers between devices, on_device(): key_piece = lax.all_gather(key_rows, 'seq', axis=0, tiled=True)  65 us
    all_gather x1, waiting for transfers between devices, on_device(): lax.all_gather(up_part, ('scene', 'seq'), axis=0, tiled=True)  63 us
    all_gather x1, waiting for transfers between devices, on_device(): lax.all_gather(qkv_part, ('scene', 'seq'), axis=0, tiled=True)  63 us
    all_gather x1, waiting for transfers between devices, on_device(): lax.all_gather(down_part, ('scene', 'seq'), axis=0, tiled=True)  59.8 us
  transfers between devices with their start and end apart: 12, of which 12 were waited for; matrix products, arithmetic and copies ran while one was open for 15% of the time, Pallas kernels for 0%

commit v1 on v0

--- a/solution.py
+++ b/solution.py
@@ -6,6 +6,16 @@
 HEADS = 12
 HEAD = 64
 NEG_BIG = -1e30
+
+
+def end_marks_over_axis(local_array, field):
+    return jnp.split(
+        lax.all_gather(
+            jnp.concatenate([local_array, field], 1), axis_name="seq", axis=0, tiled=True
+        ),
+        [local_array.shape[1]],
+        1,
+    )
 
 
 def norm_rows(values, gain_vector):
@@ -82,8 +92,7 @@
         return places % local_rows < live_count
 
     row_max = jnp.full((HEADS, local_rows), NEG_BIG, jnp.float32)
-    key_piece = lax.all_gather(key_rows, "seq", axis=0, tiled=True)
-    value_piece = lax.all_gather(value_rows, "seq", axis=0, tiled=True)
+    key_piece, value_piece = end_marks_over_axis(key_rows, value_rows)
     piece_rows = key_piece.shape[0]
     scores = (
         jnp.einsum(

time: 1150 us -> 1280 us (1.11)
  waiting for transfers between devices: 860 us -> 965 us
  local copies, waits for them, and re-layouts: 35 us -> 53.8 us
  matrix products: 156 us -> 173 us
    all_gather x0 -> x1, waiting for transfers between devices: none -> 113 us  [end_marks_over_axis(): lax.all_gather(jnp.concatenate([local_array, field], 1), axis_name='seq',...]
    unnamed x14 -> x15, waiting for transfers between devices: 92.4 us -> 114 us
    split x0 -> x3, local copies, waits for them, and re-layouts: none -> 17.9 us  [end_marks_over_axis(): jnp.split(lax.all_gather(jnp.concatenate([local_array, field], 1), axis_n...]
    dot_general x0 -> x1, matrix products: none -> 17 us  [score_grads(): jnp.einsum('qhd,khd->hqk', query_part, key_part, preferred_element_type=j...]
    all_gather x1, waiting for transfers between devices: 16.4 us -> 0.02 us  [on_device(): lax.all_gather(out_part, ('scene', 'seq'), axis=0, tiled=True)]
    all_gather x1, waiting for transfers between devices: 63 us -> 49.8 us  [on_device(): lax.all_gather(up_part, ('scene', 'seq'), axis=0, tiled=True)]
  transfers between devices with their start and end apart: 12 -> 13, of which waited for: 12 -> 12; matrix products, arithmetic and copies ran while one was open for 15% -> 15% of each run, Pallas kernels for 0% -> 0%
where the time goes in v1:
time: 1280 us
  waiting for transfers between devices  965 us (75%)
  matrix products  173 us (14%)
  local copies, waits for them, and re-layouts  53.8 us (4%)
  blocking collectives  40.4 us (3%)
  other arithmetic  28.3 us (2%)
  between operations  15.2 us (1%)
    reduce_scatter x1, waiting for transfers between devices, on_device(): lax.psum_scatter(down_grad, ('scene', 'seq'), scatter_dimension=0, tiled=...  142 us
    reduce_scatter x1, waiting for transfers between devices, on_device(): lax.psum_scatter(up_grad, ('scene', 'seq'), scatter_dimension=0, tiled=True)  141 us
    reduce_scatter x1, waiting for transfers between devices, on_device(): lax.psum_scatter(qkv_grad, ('scene', 'seq'), scatter_dimension=0, tiled=T...  125 us
    unnamed x15, waiting for transfers between devices  114 us
    all_gather x1, waiting for transfers between devices, end_marks_over_axis(): lax.all_gather(jnp.concatenate([local_array, field], 1), axis_name='seq',...  113 us
    all_gather x1, waiting for transfers between devices, on_device(): key_piece = lax.all_gather(key_rows, 'seq', axis=0, tiled=True)  63.6 us
    all_gather x1, waiting for transfers between devices, on_device(): lax.all_gather(qkv_part, ('scene', 'seq'), axis=0, tiled=True)  63 us
    all_gather x1, waiting for transfers between devices, on_device(): lax.all_gather(down_part, ('scene', 'seq'), axis=0, tiled=True)  60 us
  transfers between devices with their start and end apart: 13, of which 12 were waited for; matrix products, arithmetic and copies ran while one was open for 15% of the time, Pallas kernels for 0%

profile of v1, /device:TPU:0, one launch (start us, length us, event | category | flops | bytes accessed | tf_op | source)
XLA Modules:
  0.0 1275.6 jit_solution(11758598934167377349)
XLA Ops:
  7.2 1.6 convert_element_type.98
  8.9 1.2 convert_reduce_fusion
  10.1 1.3 fusion.37
  11.4 63.0 %all-gather.8.cloned.1.call-done = bf16[768,2304]{1,0:T(8,128)(2,1)} async-done(((bf16[24,2304]{1,0:T(8,128)(2,1)}), bf16[768,2304]{1,0:T(8,128)(2,1)}) %all-gather.8.cloned.1.call-update) | async-done | bytes 3538960 | tf_op jit(solution)/shard_map/all_gather | solution.py:74
  74.4 3.6 convolution_convert_fusion
  78.0 1.1 fusion.68
  84.5 63.6 %all-gather.18.cloned.1.call-done = bf16[2560,768]{1,0:T(8,128)(2,1)} async-done(((bf16[320,768]{1,0:T(8,128)(2,1)}), bf16[2560,768]{1,0:T(8,128)(2,1)}) %all-gather.18.cloned.1.call-update) | async-done | bytes 3932176 | tf_op jit(solution)/shard_map/all_gather | solution.py:152
  148.1 6.3 copy.35
  154.4 17.0 %fusion.70 = f32[12,320,2560]{2,1,0:T(8,128)} fusion(bf16[320,12,64]{0,2,1:T(8,128)(2,1)S(1)} %bitcast.55, bf16[2560,12,64]{0,2,1:T(8,128)(2,1)} %bitcast.51), kind=kOutput, calls=%fused_computation.96 | convolution fusion | flops 1258291200 | bytes 43745280 | tf_op jit(solution)/shard_map/qhd,khd->hqk/dot_general | solution.py:44
  171.4 48.0 %all-gather.20.cloned.1.call-done = bf16[2560,768]{1,0:T(8,128)(2,1)} async-done(((bf16[320,768]{1,0:T(8,128)(2,1)}), bf16[2560,768]{1,0:T(8,128)(2,1)}) %all-gather.20.cloned.1.call-update) | async-done | bytes 3932176 | tf_op jit(solution)/shard_map/all_gather | solution.py:153
  219.4 6.2 copy.37
  225.6 113.2 %all-gather.10.cloned.1.call-done = bf16[2560,1536]{1,0:T(8,128)(2,1)} async-done(((bf16[320,1536]{1,0:T(8,128)(2,1)}), bf16[2560,1536]{1,0:T(8,128)(2,1)}) %all-gather.10.cloned.1.call-update) | async-done | bytes 7864336 | tf_op jit(solution)/shard_map/all_gather | solution.py:13
  338.8 5.5 fusion.67
  344.3 6.2 copy.33
  350.5 17.0 %fusion = (f32[12,320]{1,0:T(8,128)S(1)}, f32[12,320,2560]{2,1,0:T(8,128)}) fusion(pred[2560]{0:T(1024)(128)(4,1)S(1)} %fusion.52, bf16[320,12,64]{0,2,1:T(8,128)(2,1)S(1)} %bitcast.56, bf16[2560,12,64]{0,2,1:T(8,128)(2,1)} %bitcast.53), kind=kOutput, calls=%fused_computation.4 | convolution fusion | flops 1287778560 | bytes 43763200 | tf_op jit(solution)/shard_map/qhd,khd->hqk/dot_general | solution.py:98
  367.5 6.2 copy.34
  373.7 18.1 %fusion.1 = f32[12,320]{1,0:T(8,128)S(1)} fusion(f32[12,320,2560]{2,1,0:T(8,128)} %get-tuple-element.22, f32[12,320]{1,0:T(8,128)S(1)} %broadcast_maximum_fusion, pred[2560]{0:T(1024)(128)(4,1)S(1)} %fusion.52), kind=kLoop, calls=%fused_computation.5 | loop fusion | flops 39317760 | bytes 39354880 | tf_op jit(solution)/shard_map/reduce_sum | solution.py:106
  391.8 15.7 %divide_convert_fusion = bf16[320,12,64]{0,2,1:T(8,128)(2,1)S(1)} fusion(bf16[2560,12,64]{0,2,1:T(8,128)(2,1)S(1)} %bitcast.61, f32[12,320,2560]{2,1,0:T(8,128)} %get-tuple-element.22, f32[12,320]{1,0:T(8,128)S(1)} %broadcast_maximum_fusion, pred[2560]{0:T(1024)(128)(4,1)S(1)} %fusion.52, f32[320,12]{0,1:T(8,128)S(1)} %bitcast.68), kind=kOutput, calls=%fused_computation.36 | convolution fusion | flops 1298104320 | bytes 43778560 | tf_op jit(solution)/shard_map/hqk,khd->hqd/dot_general | solution.py:107
  407.7 2.1 fusion.69
  410.7 49.8 %all-gather.14.cloned.1.call-done = bf16[768,3072]{1,0:T(8,128)(2,1)} async-done(((bf16[24,3072]{1,0:T(8,128)(2,1)}), bf16[768,3072]{1,0:T(8,128)(2,1)}) %all-gather.14.cloned.1.call-update) | async-done | bytes 4718608 | tf_op jit(solution)/shard_map/all_gather | solution.py:76
  460.5 6.0 fusion.66
  466.4 60.0 %all-gather.16.cloned.1.call-done = bf16[3072,768]{1,0:T(8,128)(2,1)} async-done(((bf16[96,768]{1,0:T(8,128)(2,1)}), bf16[3072,768]{1,0:T(8,128)(2,1)}) %all-gather.16.cloned.1.call-update) | async-done | bytes 4718608 | tf_op jit(solution)/shard_map/all_gather | solution.py:77
  526.5 7.4 fusion.19
  533.9 2.5 multiply_reduce_fusion.1
  537.4 1.1 copy.36
  538.4 1.4 multiply_reduce_fusion
  539.9 26.1 %multiply_convert_fusion = bf16[12,320,2560]{2,1,0:T(8,128)(2,1)} fusion(f32[12,320,2560]{2,1,0:T(8,128)} %fusion.70, bf16[320,12,64]{0,2,1:T(8,128)(2,1)} %bitcast.66, bf16[2560,12,64]{0,2,1:T(8,128)(2,1)} %bitcast.60, f32[12,320]{1,0:T(8,128)S(1)} %bitcast.69, f32[12,320]{1,0:T(8,128)} %log_add_fusion, pred[2560]{0:T(1024)(128)(4,1)S(1)} %fusion.52), kind=kOutput, calls=%fused_computation | convolution fusion | flops 1317273600 | bytes 63439360 | tf_op jit(solution)/shard_map/qhd,khd->hqk/dot_general | solution.py:47
  565.9 12.4 multiply_convert_fusion.1
  578.3 6.2 copy.38
  585.6 18.3 %fusion.10 = bf16[12,64,2560]{2,1,0:T(8,128)(2,1)} fusion(bf16[320,12,64]{0,2,1:T(8,128)(2,1)S(1)} %bitcast.67, f32[12,320,2560]{2,1,0:T(8,128)} %fusion.70, f32[12,320]{1,0:T(8,128)S(1)} %copy-done.20, pred[2560]{0:T(1024)(128)(4,1)S(1)} %fusion.52), kind=kOutput, calls=%fused_computation.15 | convolution fusion | flops 1299578880 | bytes 43763200 | tf_op jit(solution)/shard_map/hqk,qhd->khd/dot_general | solution.py:171
  603.9 6.3 copy.40
  611.3 2.2 fusion.43
  613.6 8.7 fusion.46
  622.4 6.9 fusion.65
  629.4 11.1 fusion.24
  640.4 27.4 %reduce-scatter.19.cloned.1.call-done = bf16[320,768]{1,0:T(8,128)(2,1)} async-done(((bf16[2560,768]{1,0:T(8,128)(2,1)}), bf16[320,768]{1,0:T(8,128)(2,1)}) %reduce-scatter.19.cloned.1.call-update) | async-done | bytes 491536
  667.9 2.1 copy.39
  669.9 86.1 %reduce-scatter.21.cloned.1.call-done = bf16[320,768]{1,0:T(8,128)(2,1)} async-done(((bf16[2560,768]{1,0:T(8,128)(2,1)}), bf16[320,768]{1,0:T(8,128)(2,1)}) %reduce-scatter.21.cloned.1.call-update) | async-done | bytes 491536
  756.1 2.1 copy.41
  758.1 6.4 fusion.39
  764.6 6.9 fusion.23
  771.5 1.9 fusion.36
  773.4 40.4 %all-reduce.2 = (f32[768]{0:T(1024)S(1)}, f32[768]{0:T(1024)S(1)}) all-reduce(f32[768]{0:T(1024)S(1)} %get-tuple-element.10, f32[768]{0:T(1024)S(1)} %copy-done.24), channel_id=8, replica_groups=mesh['scene'=4,'seq'=8] {'scene','seq'}, use_global_device_ids=true, to_apply=%region_18.19.clone | all-reduce | flops 1536 | bytes 12288
  815.0 1.3 fusion.35
  816.3 44.3 %reduce-scatter.13.cloned.1.call-done = f32[24,768]{1,0:T(8,128)} async-done(((f32[768,768]{1,0:T(8,128)}), f32[24,768]{1,0:T(8,128)}) %reduce-scatter.13.cloned.1.call-update) | async-done | bytes 73744 | tf_op jit(solution)/shard_map/reduce_scatter | solution.py:202
  860.6 142.0 %reduce-scatter.17.cloned.1.call-done = f32[96,768]{1,0:T(8,128)} async-done(((f32[3072,768]{1,0:T(8,128)}), f32[96,768]{1,0:T(8,128)}) %reduce-scatter.17.cloned.1.call-update) | async-done | bytes 294928 | tf_op jit(solution)/shard_map/reduce_scatter | solution.py:204
  1002.7 140.9 %reduce-scatter.15.cloned.1.call-done = f32[24,3072]{1,0:T(8,128)} async-done(((f32[768,3072]{1,0:T(8,128)}), f32[24,3072]{1,0:T(8,128)}) %reduce-scatter.15.cloned.1.call-update) | async-done | bytes 294928 | tf_op jit(solution)/shard_map/reduce_scatter | solution.py:203
  1143.6 125.2 %reduce-scatter.11.cloned.1.call-done = f32[24,2304]{1,0:T(8,128)} async-done(((f32[768,2304]{1,0:T(8,128)}), f32[24,2304]{1,0:T(8,128)}) %reduce-scatter.11.cloned.1.call-update) | async-done | bytes 221200 | tf_op jit(solution)/shard_map/reduce_scatter | solution.py:201
  (102 shorter events, 10.2 us)
Async XLA Ops:
  7.2 67.2 %all-gather.8.cloned.1.call-start = ((), (), s32[]{:S(2)}) async-start(), calls=%async_computation.6 | async-start | bytes 3649536 | tf_op jit(solution)/shard_map/all_gather | solution.py:74
  8.8 139.3 %all-gather.18.cloned.1.call-start = ((), (), s32[]{:S(2)}) async-start(), calls=%async_computation.11 | async-start | bytes 4423680 | tf_op jit(solution)/shard_map/all_gather | solution.py:152
  10.1 64.3 %copy-start.16 = (f32[320]{0:T(512)}, f32[320]{0:T(512)S(1)}, u32[]{:S(2)}) copy-start(f32[320]{0:T(512)S(1)} %broadcast_multiply_fusion.5) | copy-start | bytes 3844
  11.4 63.0 %copy-start.18 = (f32[320]{0:T(512)}, f32[320]{0:T(512)S(1)}, u32[]{:S(2)}) copy-start(f32[320]{0:T(512)S(1)} %add_rsqrt_fusion.1) | copy-start | bytes 3844
  78.0 3.0 copy-start.15
  78.0 3.7 copy-start.11
  78.0 4.4 copy-start.12
  79.1 140.3 %all-gather.20.cloned.1.call-start = ((), (), s32[]{:S(2)}) async-start(), calls=%async_computation.12 | async-start | bytes 4423680 | tf_op jit(solution)/shard_map/all_gather | solution.py:153
  79.8 259.0 %all-gather.10.cloned.1.call-start = ((), (), s32[]{:S(2)}) async-start(), calls=%async_computation.7 | async-start | bytes 8847360 | tf_op jit(solution)/shard_map/all_gather | solution.py:13
  80.9 326.7 %all-gather.12.cloned.1.call-start = ((), (), s32[]{:S(2)}) async-start(), calls=%async_computation.8 | async-start | bytes 1216512 | tf_op jit(solution)/shard_map/all_gather | solution.py:75
  81.6 378.8 %all-gather.14.cloned.1.call-start = ((), (), s32[]{:S(2)}) async-start(), calls=%async_computation.9 | async-start | bytes 4866048 | tf_op jit(solution)/shard_map/all_gather | solution.py:76
  82.4 444.1 %all-gather.16.cloned.1.call-start = ((), (), s32[]{:S(2)}) async-start(), calls=%async_computation.10 | async-start | bytes 4866048 | tf_op jit(solution)/shard_map/all_gather | solution.py:77
  83.1 584.7 %reduce-scatter.19.cloned.1.call-start = ((), (), s32[]{:S(2)}) async-start(), calls=%async_computation.17 | async-start | bytes 4423680
  84.1 442.3 %copy-start.21 = (f32[320]{0:T(512)}, f32[320]{0:T(512)S(1)}, u32[]{:S(2)}) copy-start(f32[320]{0:T(512)S(1)} %fusion.56) | copy-start | bytes 3844
  373.7 18.1 %copy-start.4 = (bf16[2560,768]{0,1:T(8,128)(2,1)S(1)}, bf16[2560,768]{0,1:T(8,128)(2,1)}, u32[]{:S(2)}) copy-start(bf16[2560,768]{0,1:T(8,128)(2,1)} %copy.34) | copy-start | bytes 11796484
  391.8 15.8 %copy-start = (bf16[320,768]{1,0:T(8,128)(2,1)S(1)}, bf16[320,768]{1,0:T(8,128)(2,1)}, u32[]{:S(2)}) copy-start(bf16[320,768]{1,0:T(8,128)(2,1)} %param.9) | copy-start | bytes 1474564
  407.6 58.8 %copy-start.1 = (bf16[320,12,64]{0,2,1:T(8,128)(2,1)}, bf16[320,12,64]{0,2,1:T(8,128)(2,1)S(1)}, u32[]{:S(2)}) copy-start(bf16[320,12,64]{0,2,1:T(8,128)(2,1)S(1)} %divide_convert_fusion) | copy-start | bytes 1474564
  407.6 52.9 %copy-start.13 = (f32[768]{0:T(1024)S(1)}, f32[768]{0:T(1024)}, u32[]{:S(2)}) copy-start(f32[768]{0:T(1024)} %param.17) | copy-start | bytes 9220
  410.7 115.8 %copy-start.9 = (bf16[320,768]{1,0:T(8,128)(2,1)S(1)}, bf16[320,768]{1,0:T(8,128)(2,1)}, u32[]{:S(2)}) copy-start(bf16[320,768]{1,0:T(8,128)(2,1)} %param.11) | copy-start | bytes 1474564
  526.5 7.4 copy-start.25
  533.8 2.5 copy-start.8
  533.8 2.5 copy-start.22
  533.9 2.9 copy-start.3
  584.5 1.1 copy-start.7
  584.5 1.1 copy-start.20
  584.6 171.5 %reduce-scatter.21.cloned.1.call-start = ((), (), s32[]{:S(2)}) async-start(), calls=%async_computation.18 | async-start | bytes 4423680
  610.2 1.1 copy-start.2
  610.3 3.3 copy-start.10
  610.3 3.3 copy-start.23
  610.3 250.3 %reduce-scatter.13.cloned.1.call-start = ((), (), s32[]{:S(2)}) async-start(), calls=%async_computation.14 | async-start | bytes 2433024 | tf_op jit(solution)/shard_map/reduce_scatter | solution.py:202
  613.5 389.1 %reduce-scatter.17.cloned.1.call-start = ((), (), s32[]{:S(2)}) async-start(), calls=%async_computation.16 | async-start | bytes 9732096 | tf_op jit(solution)/shard_map/reduce_scatter | solution.py:204
  622.3 521.3 %reduce-scatter.15.cloned.1.call-start = ((), (), s32[]{:S(2)}) async-start(), calls=%async_computation.15 | async-start | bytes 9732096 | tf_op jit(solution)/shard_map/reduce_scatter | solution.py:203
  629.3 128.9 %copy-start.14 = (f32[768]{0:T(1024)S(1)}, f32[768]{0:T(1024)}, u32[]{:S(2)}) copy-start(f32[768]{0:T(1024)} %param.16) | copy-start | bytes 9220
  629.3 128.9 %copy-start.17 = (f32[320]{0:T(512)S(1)}, f32[320]{0:T(512)}, u32[]{:S(2)}) copy-start(f32[320]{0:T(512)} %copy-done.16) | copy-start | bytes 3844
  629.3 128.8 %copy-start.19 = (f32[320]{0:T(512)S(1)}, f32[320]{0:T(512)}, u32[]{:S(2)}) copy-start(f32[320]{0:T(512)} %copy-done.18) | copy-start | bytes 3844
  629.3 639.5 %reduce-scatter.11.cloned.1.call-start = ((), (), s32[]{:S(2)}) async-start(), calls=%async_computation.13 | async-start | bytes 7299072 | tf_op jit(solution)/shard_map/reduce_scatter | solution.py:201
  764.6 6.9 copy-start.5
  764.6 6.9 copy-start.6
  764.6 6.9 copy-start.26
  771.5 1.9 copy-start.24
Sparse Core Ops, SparseCore 0:
  11.5 62.8 all-gather.7
  79.2 68.8 all-gather.17
  150.9 68.4 all-gather.19
  222.0 116.7 all-gather.9
  342.1 52.2 all-gather.11
  397.8 62.6 all-gather.13
  463.9 62.4 all-gather.15
  584.7 83.1 reduce-scatter.18
  672.0 84.0 reduce-scatter.20
  761.8 98.8 reduce-scatter.12
  868.1 134.5 reduce-scatter.16
  1009.0 134.5 reduce-scatter.14
  1150.8 117.9 reduce-scatter.10
